TPU v7x, 32 devices: a whole 2x2x4 slice. The times are simulated.
32 devices in a mesh: wide: 8 (over z, x), narrow: 4 (over y, core).
Axes of the slice: x: 2, y: 2, z: 4, core: 2. Of those that a mesh axis runs over, the one named last changes fastest.
Arguments:
- block_source: bfloat16 [64, 576, 384], P(('wide', 'narrow')), may hold values from -6 to 6
- upstream_adjoint: bfloat16 [64, 576, 384], P(('wide', 'narrow')), may hold values from -6 to 6
- picture_patch_extents: int32 [64, 2], P(('wide', 'narrow')), may hold values from 18 to 24, as said below
- triple_matrix: float32 [384, 1152], replicated, may hold values from -0.3125 to 0.3125
- mixer_matrix: float32 [384, 384], replicated, may hold values from -1.25 to 1.25
- expand_matrix: float32 [384, 1536], replicated, may hold values from -0.3125 to 0.3125
- shrink_matrix: float32 [1536, 384], replicated, may hold values from -0.15625 to 0.15625
- affine_entries: float32 [40, 384], replicated, may hold values from -2 to 2
- sharpness: float32 [8], replicated, may hold values from 10 to 30
- triple_velocity: float32 [384, 1152], P(None, 'narrow'), may hold values from -100 to 100
- mixer_velocity: float32 [384, 384], P('narrow'), may hold values from -300 to 300
- expand_velocity: float32 [384, 1536], P(None, 'narrow'), may hold values from -500 to 500
- shrink_velocity: float32 [1536, 384], P('narrow'), may hold values from -500 to 500
- affine_velocity: float32 [40, 384], replicated, may hold values from -300 to 300
- sharpness_velocity: float32 [8], replicated, may hold values from -8 to 8
Outputs:
- block_out: bfloat16 [64, 576, 384], P(('wide', 'narrow'))
- incoming_adjoint: float32 [64, 576, 384], P(('wide', 'narrow'))
- triple_matrix_adjoint: float32 [384, 1152], P(None, 'narrow')
- mixer_matrix_adjoint: float32 [384, 384], P('narrow')
- expand_matrix_adjoint: float32 [384, 1536], P(None, 'narrow')
- shrink_matrix_adjoint: float32 [1536, 384], P('narrow')
- affine_entries_adjoint: float32 [40, 384], replicated
- sharpness_adjoint: float32 [8], replicated
- revised_triple_matrix: float32 [384, 1152], P(None, 'narrow')
- revised_mixer_matrix: float32 [384, 384], P('narrow')
- revised_expand_matrix: float32 [384, 1536], P(None, 'narrow')
- revised_shrink_matrix: float32 [1536, 384], P('narrow')
- renewed_triple_velocity: float32 [384, 1152], P(None, 'narrow')
- renewed_mixer_velocity: float32 [384, 384], P('narrow')
- renewed_expand_velocity: float32 [384, 1536], P(None, 'narrow')
- renewed_shrink_velocity: float32 [1536, 384], P('narrow')
- copy_qkv: bfloat16 [384, 1152], P(None, 'narrow')
- copy_proj: bfloat16 [384, 384], P('narrow')
- copy_fc1: bfloat16 [384, 1536], P(None, 'narrow')
- copy_fc2: bfloat16 [1536, 384], P('narrow')
- revised_affine_entries: float32 [40, 384], replicated
- renewed_affine_velocity: float32 [40, 384], replicated
- revised_sharpness: float32 [8], replicated
- renewed_sharpness_velocity: float32 [8], replicated
Inputs may be any that keep to these rules, and one draw needn't show every extreme that they name: Image i holds real patches in the top-left picture_patch_extents[i, 0] x picture_patch_extents[i, 1] block of its 24 x 24 slots; some image fills all its slots in every draw.
All inputs are finite; a program needn't handle non-finite values.
Results may differ from a plain program's by a relative error of at most 0.006.
The roundings to bfloat16 on the way count: a program that leaves them out, or rounds other values in their place, can miss the bound.
Values sent between devices are 32-bit elements; how exact they have to be, the bound alone decides.
No kernel may reach another device: no remote copies, remote signals or barrier semaphores. Data moves between devices by JAX's collectives and lax.ppermute only.
A program may use at most 128 MiB of HBM per device.

v0:
```python
import math

import jax
import jax.numpy as jnp
from jax import lax
from jax.sharding import PartitionSpec as P

GRID = 24
NS_STEPS = 5


highest = lax.Precision.HIGHEST
layer_eps = 1e-06
unit_eps = 1e-06
batch_eps = 1e-05
frob_eps = 1e-07
velocity_damping = 0.5
rate_matrix = 0.25
affine_step_size = 0.2
coef_first = 3.4445
coef_second = -4.775
coef_third = 2.0315
root_half = 0.7071067811865476
inverse_root_tau = 0.3989422804014327


def layer_stats(source, gain_row, bias_row):
    centre = source - jnp.mean(source, axis=-1, keepdims=True)
    inverse = lax.rsqrt(jnp.mean(centre * centre, axis=-1, keepdims=True) + layer_eps)
    normal = centre * inverse
    return (normal * gain_row + bias_row, normal, inverse)


def layer_back(grad_norm, normal, inverse, gain_row):
    scaled = grad_norm * gain_row
    return inverse * (
        scaled
        - jnp.mean(scaled, axis=-1, keepdims=True)
        - normal * jnp.mean(scaled * normal, axis=-1, keepdims=True)
    )


def token_sum(source):
    return jnp.sum(source, axis=(0, 1))


def gelu_exact(source):
    return 0.5 * source * (1.0 + lax.erf(source * root_half))


def gelu_slope(source):
    return (
        0.5 * (1.0 + lax.erf(source * root_half))
        + source * jnp.exp(-0.5 * source * source) * inverse_root_tau
    )


def depthwise(source, kernel):
    grid_side = source.shape[1]
    padded = jnp.pad(source, ((0, 0), (1, 1), (1, 1), (0, 0)))
    summed = jnp.zeros_like(source)
    for offset in range(9):
        summed = (
            summed
            + padded[
                :, offset // 3 : offset // 3 + grid_side, offset % 3 : offset % 3 + grid_side, :
            ]
            * kernel[offset]
        )
    return summed


def kernel_grad(source, grad_conv):
    grid_side = source.shape[1]
    padded = jnp.pad(source, ((0, 0), (1, 1), (1, 1), (0, 0)))
    return jnp.stack(
        [
            jnp.sum(
                padded[
                    :, offset // 3 : offset // 3 + grid_side, offset % 3 : offset % 3 + grid_side, :
                ]
                * grad_conv,
                axis=(0, 1, 2),
            )
            for offset in range(9)
        ]
    )


def unit_back(grad_unit, unit_vals, inverse):
    return inverse * (grad_unit - unit_vals * jnp.sum(grad_unit * unit_vals, axis=1, keepdims=True))


def right_mul(left, right):
    return jnp.einsum("gsk,ke->gse", left, right, preferred_element_type=jnp.float32)


def right_mul_t(left, right):
    return jnp.einsum("gse,ke->gsk", left, right, preferred_element_type=jnp.float32)


def outer_sum(left, right):
    return jnp.einsum("gsk,gse->ke", left, right, preferred_element_type=jnp.float32)


def local_gram(source, is_tall):
    if is_tall:
        return jnp.dot(source.T, source, precision=highest)
    return jnp.dot(source, source.T, precision=highest)


def gram_sum(fields, tall_flags):
    return lax.psum(
        (
            local_gram(fields[0], tall_flags[0]),
            local_gram(fields[1], tall_flags[1]),
            local_gram(fields[2], tall_flags[2]),
            local_gram(fields[3], tall_flags[3]),
        ),
        "narrow",
    )


def polish(source, gram_now, is_tall):
    polynomial = coef_second * gram_now + coef_third * jnp.dot(
        gram_now, gram_now, precision=highest
    )
    if is_tall:
        return coef_first * source + jnp.dot(source, polynomial, precision=highest)
    return coef_first * source + jnp.dot(polynomial, source, precision=highest)


def on_device(
    block_source,
    upstream_adjoint,
    picture_patch_extents,
    triple_matrix,
    mixer_matrix,
    expand_matrix,
    shrink_matrix,
    affine_entries,
    sharpness,
    triple_velocity,
    mixer_velocity,
    expand_velocity,
    shrink_velocity,
    affine_velocity,
    sharpness_velocity,
):
    images, slot_count, model_width = block_source.shape
    group_index = sharpness.shape[0]
    head_size = model_width // group_index
    grid_side = GRID
    flat_shape = block_source.shape
    grid_shape = (images, grid_side, grid_side, model_width)
    head_shape = (images, slot_count, group_index, head_size)
    position = jnp.arange(slot_count, dtype=jnp.int32)
    rows_ok = (position // grid_side)[None, :] < picture_patch_extents[:, 0:1]
    cols_ok = (position % grid_side)[None, :] < picture_patch_extents[:, 1:2]
    interior_patches = (rows_ok & cols_ok).astype(jnp.float32)
    inside_col = interior_patches[:, :, None]
    asker_lowprec = triple_matrix.astype(jnp.bfloat16)
    attention_weights_lowprec = mixer_matrix.astype(jnp.bfloat16)
    one_low = expand_matrix.astype(jnp.bfloat16)
    two_low = shrink_matrix.astype(jnp.bfloat16)
    incoming_patches = block_source.astype(jnp.float32)
    norm_one, unit_one, inv_one = layer_stats(
        incoming_patches, affine_entries[0], affine_entries[1]
    )
    norm_one_low = norm_one.astype(jnp.bfloat16)
    joined = right_mul(norm_one_low, asker_lowprec) + affine_entries[2:5].reshape(-1)
    query_in = joined[:, :, :model_width] * inside_col
    key_in = joined[:, :, model_width : 2 * model_width] * inside_col
    value_heads = joined[:, :, 2 * model_width :].reshape(head_shape)
    query_inv = lax.rsqrt(jnp.sum(query_in * query_in, axis=1, keepdims=True) + unit_eps)
    key_inv = lax.rsqrt(jnp.sum(key_in * key_in, axis=1, keepdims=True) + unit_eps)
    query_unit = query_in * query_inv
    key_unit = key_in * key_inv
    query_heads = query_unit.reshape(head_shape)
    key_heads = key_unit.reshape(head_shape)
    feature_crosscov = jnp.einsum("gshi,gshj->ghij", query_heads, key_heads, precision=highest)
    mix_patches = jax.nn.softmax(feature_crosscov * sharpness[None, :, None, None], axis=-1)
    mixing_low = (
        jnp.einsum("ghij,gshj->gshi", mix_patches, value_heads, precision=highest)
        .reshape(flat_shape)
        .astype(jnp.bfloat16)
    )
    branch_one = right_mul(mixing_low, attention_weights_lowprec) + affine_entries[5]
    after_mix = incoming_patches + inside_col * affine_entries[6] * branch_one
    norm_two, unit_two, inv_two = layer_stats(after_mix, affine_entries[7], affine_entries[8])
    local_in = (norm_two * inside_col).reshape(grid_shape)
    conv_one = depthwise(local_in, affine_entries[9:18]).reshape(flat_shape) + affine_entries[18]
    activated = gelu_exact(conv_one)
    local_count = jnp.sum(interior_patches)
    first_sums = lax.psum((token_sum(activated * inside_col), local_count), ("wide", "narrow"))
    genuine_patch_tally = first_sums[1]
    centre_mean = first_sums[0] / genuine_patch_tally
    deviation = (activated - centre_mean) * inside_col
    variance = lax.psum(token_sum(deviation * deviation), ("wide", "narrow")) / genuine_patch_tally
    inverse_std = lax.rsqrt(variance + batch_eps)
    unit_bn = (activated - centre_mean) * inverse_std * inside_col
    normal_bn = (unit_bn * affine_entries[19] + affine_entries[20]) * inside_col
    normal_grid = normal_bn.reshape(grid_shape)
    conv_two = (
        depthwise(normal_grid, affine_entries[21:30]).reshape(flat_shape) + affine_entries[30]
    )
    after_local = after_mix + inside_col * affine_entries[31] * conv_two
    norm_three, unit_three, inv_three = layer_stats(
        after_local, affine_entries[32], affine_entries[33]
    )
    norm_three_low = norm_three.astype(jnp.bfloat16)
    hidden = right_mul(norm_three_low, one_low) + affine_entries[34:38].reshape(-1)
    hidden_low = gelu_exact(hidden).astype(jnp.bfloat16)
    branch_three = right_mul(hidden_low, two_low) + affine_entries[38]
    block_out = (after_local + inside_col * affine_entries[39] * branch_three).astype(jnp.bfloat16)
    grad_out = upstream_adjoint.astype(jnp.float32)
    grad_branch3 = (inside_col * affine_entries[39] * grad_out).astype(jnp.bfloat16)
    gamma_three = token_sum(inside_col * grad_out * branch_three)
    bias_fc2 = token_sum(grad_branch3.astype(jnp.float32))
    grad_w2 = outer_sum(hidden_low, grad_branch3)
    grad_hidden = (right_mul_t(grad_branch3, two_low) * gelu_slope(hidden)).astype(jnp.bfloat16)
    bias_fc1 = token_sum(grad_hidden.astype(jnp.float32)).reshape(4, model_width)
    grad_w1 = outer_sum(norm_three_low, grad_hidden)
    grad_norm3 = right_mul_t(grad_hidden, one_low)
    gain_three = token_sum(grad_norm3 * unit_three)
    shift_three = token_sum(grad_norm3)
    grad_local = grad_out + layer_back(grad_norm3, unit_three, inv_three, affine_entries[32])
    grad_conv2 = inside_col * affine_entries[31] * grad_local
    gamma_two = token_sum(inside_col * grad_local * conv_two)
    bias_conv2 = token_sum(grad_conv2)
    grad_conv2_grid = grad_conv2.reshape(grid_shape)
    kernel_two = kernel_grad(normal_grid, grad_conv2_grid)
    grad_bn = depthwise(grad_conv2_grid, affine_entries[29:20:-1]).reshape(flat_shape) * inside_col
    bn_grads = lax.psum((token_sum(grad_bn), token_sum(grad_bn * unit_bn)), ("wide", "narrow"))
    bias_bn = bn_grads[0]
    gain_bn = bn_grads[1]
    grad_act = (
        inside_col
        * affine_entries[19]
        * inverse_std
        * (grad_bn - (bias_bn + unit_bn * gain_bn) / genuine_patch_tally)
    )
    grad_conv1 = grad_act * gelu_slope(conv_one)
    bias_conv1 = token_sum(grad_conv1)
    grad_conv1_grid = grad_conv1.reshape(grid_shape)
    kernel_one = kernel_grad(local_in, grad_conv1_grid)
    grad_norm2 = (
        depthwise(grad_conv1_grid, affine_entries[17:8:-1]).reshape(flat_shape) * inside_col
    )
    gain_two = token_sum(grad_norm2 * unit_two)
    shift_two = token_sum(grad_norm2)
    grad_mix = grad_local + layer_back(grad_norm2, unit_two, inv_two, affine_entries[7])
    grad_branch1 = (inside_col * affine_entries[6] * grad_mix).astype(jnp.bfloat16)
    gamma_one = token_sum(inside_col * grad_mix * branch_one)
    bias_proj = token_sum(grad_branch1.astype(jnp.float32))
    grad_wp = outer_sum(mixing_low, grad_branch1)
    grad_mixing = right_mul_t(grad_branch1, attention_weights_lowprec).reshape(head_shape)
    grad_attend = jnp.einsum("gshi,gshj->ghij", grad_mixing, value_heads, precision=highest)
    grad_value = jnp.einsum("ghij,gshi->gshj", mix_patches, grad_mixing, precision=highest).reshape(
        flat_shape
    )
    logits_adjoint = mix_patches * (
        grad_attend - jnp.sum(mix_patches * grad_attend, axis=-1, keepdims=True)
    )
    sharpness_adjoint = jnp.sum(logits_adjoint * feature_crosscov, axis=(0, 2, 3))
    crosscov_adjoint = logits_adjoint * sharpness[None, :, None, None]
    grad_qunit = jnp.einsum(
        "ghij,gshj->gshi", crosscov_adjoint, key_heads, precision=highest
    ).reshape(flat_shape)
    grad_kunit = jnp.einsum(
        "ghij,gshi->gshj", crosscov_adjoint, query_heads, precision=highest
    ).reshape(flat_shape)
    grad_query = unit_back(grad_qunit, query_unit, query_inv) * inside_col
    grad_key = unit_back(grad_kunit, key_unit, key_inv) * inside_col
    grad_joined = jnp.concatenate([grad_query, grad_key, grad_value], axis=-1).astype(jnp.bfloat16)
    bias_qkv = token_sum(grad_joined.astype(jnp.float32)).reshape(3, model_width)
    grad_wq = outer_sum(norm_one_low, grad_joined)
    grad_norm1 = right_mul_t(grad_joined, asker_lowprec)
    gain_one = token_sum(grad_norm1 * unit_one)
    shift_one = token_sum(grad_norm1)
    incoming_adjoint = grad_mix + layer_back(grad_norm1, unit_one, inv_one, affine_entries[0])
    zero_row = jnp.zeros((model_width,), jnp.float32)
    grad_vec = jnp.concatenate(
        [
            jnp.stack([gain_one, shift_one]),
            bias_qkv,
            jnp.stack([bias_proj, gamma_one, gain_two, shift_two]),
            kernel_one,
            jnp.stack([bias_conv1, zero_row, zero_row]),
            kernel_two,
            jnp.stack([bias_conv2, gamma_two, gain_three, shift_three]),
            bias_fc1,
            jnp.stack([bias_fc2, gamma_three]),
        ]
    )
    narrow_parts = lax.axis_size("narrow")
    narrow_pos = lax.axis_index("narrow")

    def own_part(full_matrix, along):
        part_size = full_matrix.shape[along] // narrow_parts
        return lax.dynamic_slice_in_dim(full_matrix, narrow_pos * part_size, part_size, along)

    summed = lax.psum(
        (grad_wq, grad_wp, grad_w1, grad_w2, grad_vec, sharpness_adjoint), ("wide", "narrow")
    )
    shard_grads = (
        own_part(summed[0], 1),
        own_part(summed[1], 0),
        own_part(summed[2], 1),
        own_part(summed[3], 0),
    )
    vec_total = summed[4]
    sharpness_sum = summed[5]
    vec_full = jnp.concatenate([vec_total[:19], jnp.stack([gain_bn, bias_bn]), vec_total[21:]])
    tall_flags = (
        triple_matrix.shape[0] >= triple_matrix.shape[1],
        mixer_matrix.shape[0] >= mixer_matrix.shape[1],
        expand_matrix.shape[0] >= expand_matrix.shape[1],
        shrink_matrix.shape[0] >= shrink_matrix.shape[1],
    )
    moments = (triple_velocity, mixer_velocity, expand_velocity, shrink_velocity)
    states = [velocity_damping * moments[member] + shard_grads[member] for member in range(4)]

    def gram_list(fields):
        return gram_sum(fields, tall_flags)

    raw_grams = gram_list(states)
    norms = [jnp.sqrt(jnp.trace(raw_grams[member])) + frob_eps for member in range(4)]
    fields = [states[member] / norms[member] for member in range(4)]
    gram_set = [raw_grams[member] / (norms[member] * norms[member]) for member in range(4)]
    for sweep_index in range(NS_STEPS):
        if sweep_index > 0:
            gram_set = gram_list(fields)
        fields = [
            polish(fields[member], gram_set[member], tall_flags[member]) for member in range(4)
        ]
    full_weights = (triple_matrix, mixer_matrix, expand_matrix, shrink_matrix)
    factors = [
        math.sqrt(max(1.0, full_weights[member].shape[0] / full_weights[member].shape[1]))
        for member in range(4)
    ]
    masters = (
        own_part(triple_matrix, 1),
        own_part(mixer_matrix, 0),
        own_part(expand_matrix, 1),
        own_part(shrink_matrix, 0),
    )
    new_masters = [
        masters[member] - rate_matrix * factors[member] * fields[member] for member in range(4)
    ]
    vec_state = velocity_damping * affine_velocity + vec_full
    new_vec = affine_entries - affine_step_size * vec_state * lax.rsqrt(genuine_patch_tally)
    sharpness_buffer = velocity_damping * sharpness_velocity + sharpness_sum
    sharpness_following = sharpness - affine_step_size * sharpness_buffer * lax.rsqrt(
        genuine_patch_tally
    )
    return (
        block_out,
        incoming_adjoint,
        shard_grads[0],
        shard_grads[1],
        shard_grads[2],
        shard_grads[3],
        vec_full,
        sharpness_sum,
        new_masters[0],
        new_masters[1],
        new_masters[2],
        new_masters[3],
        states[0],
        states[1],
        states[2],
        states[3],
        new_masters[0].astype(jnp.bfloat16),
        new_masters[1].astype(jnp.bfloat16),
        new_masters[2].astype(jnp.bfloat16),
        new_masters[3].astype(jnp.bfloat16),
        new_vec,
        vec_state,
        sharpness_following,
        sharpness_buffer,
    )


def solution(mesh):
    return jax.shard_map(
        on_device,
        mesh=mesh,
        in_specs=(
            P(("wide", "narrow"), None, None),
            P(("wide", "narrow"), None, None),
            P(("wide", "narrow"), None),
            P(),
            P(),
            P(),
            P(),
            P(),
            P(),
            P(None, "narrow"),
            P("narrow", None),
            P(None, "narrow"),
            P("narrow", None),
            P(),
            P(),
        ),
        out_specs=(
            P(("wide", "narrow"), None, None),
            P(("wide", "narrow"), None, None),
            P(None, "narrow"),
            P("narrow", None),
            P(None, "narrow"),
            P("narrow", None),
            P(),
            P(),
            P(None, "narrow"),
            P("narrow", None),
            P(None, "narrow"),
            P("narrow", None),
            P(None, "narrow"),
            P("narrow", None),
            P(None, "narrow"),
            P("narrow", None),
            P(None, "narrow"),
            P("narrow", None),
            P(None, "narrow"),
            P("narrow", None),
            P(),
            P(),
            P(),
            P(),
        ),
        check_vma=False,
    )
```

profile of v0, /device:TPU:0, one launch (start us, length us, event | category | flops | bytes accessed | tf_op | source)
XLA Modules:
  0.0 852.0 jit_solution(10013970673999232989)
XLA Ops:
  16.7 3.2 convolution_add_fusion
  20.5 2.9 fusion.74
  25.5 3.5 copy.57
  29.0 2.8 copy.55
  31.8 4.0 multiply_reduce_fusion.39
  41.8 4.1 multiply_reduce_fusion.30
  45.9 42.3 %all-reduce.6 = (f32[384]{0:T(512)}, f32[]{:T(128)}) all-reduce(f32[384]{0:T(512)} %get-tuple-element.154, f32[]{:T(128)} %get-tuple-element.152), channel_id=1, replica_groups=mesh['wide'=8,'narrow'=4] {'wide','narrow'}, use_global_device_ids=true, to_apply=%region_9.10 | all-reduce | flops 385 | bytes 3080 | tf_op jit(solution)/shard_map/psum | solution.py:195
  90.1 2.5 multiply_reduce_fusion.29
  92.6 41.0 %psum.219 = f32[384]{0:T(512)} all-reduce(f32[384]{0:T(512)} %multiply_reduce_fusion.29), channel_id=1, replica_groups=mesh['wide'=8,'narrow'=4] {'wide','narrow'}, use_global_device_ids=true, to_apply=%region_13.14 | all-reduce | flops 384 | bytes 3072 | tf_op jit(solution)/shard_map/psum | solution.py:199
  144.1 6.3 multiply_convert_fusion
  150.4 5.4 convert_reduce_fusion
  155.9 3.3 convolution_bitcast_fusion.1
  159.2 3.0 multiply_reduce_fusion
  162.3 2.5 fusion.168
  165.0 4.3 fusion.167
  169.2 40.5 %all-reduce.5 = (f32[384]{0:T(512)}, f32[384]{0:T(512)}) all-reduce(f32[384]{0:T(512)} %get-tuple-element.58, f32[384]{0:T(512)} %get-tuple-element.57), channel_id=1, replica_groups=mesh['wide'=8,'narrow'=4] {'wide','narrow'}, use_global_device_ids=true, to_apply=%region_21.22 | all-reduce | flops 768 | bytes 6144 | tf_op jit(solution)/shard_map/psum | solution.py:234
  209.8 11.9 %multiply_reduce_fusion.11 = (f32[384]{0:T(512)}, f32[384]{0:T(512)}, f32[384]{0:T(512)}, f32[384]{0:T(512)}, f32[384]{0:T(512)}, /*index=5*/f32[384]{0:T(512)},...) fusion(f32[2,24,24,384]{3,2,1,0:T(8,128)} %bitcast.199, ...), kind=kLoop, calls=%fused_computation.137 | loop fusion | flops 16806144 | bytes 8875012 | tf_op jit(solution)/shard_map/reduce_sum | solution.py:78
  221.8 3.2 multiply_reduce_fusion.34
  229.9 8.0 fusion.28
  240.5 2.4 multiply_reduce_fusion.38
  242.9 3.4 fusion.132
  246.3 3.2 fusion.130
  249.6 2.9 convolution_convert_fusion
  254.0 3.7 convolution_bitcast_fusion
  257.7 3.1 copy.63
  260.8 3.4 multiply_convert_fusion.2
  264.2 3.0 copy.65
  267.2 3.4 multiply_convert_fusion.1
  272.4 4.6 convolution_bitcast_fusion.2
  277.1 165.2 %all-reduce.20.cloned.1.call-done = (f32[384,1152]{0,1:T(8,128)}, f32[384,384]{1,0:T(8,128)}, f32[384,1536]{1,0:T(8,128)}, f32[1536,384]{1,0:T(8,128)}) async-done(((f32[384,1152]{0,1:T(8,128)}, f32[384,384]{1,0:T(8,128)}, f32[384,1536]{1,0:T(8,128)}, f32[1536,384]{1,0:T(8,128)}), (f32[384,1152]{0,1:T(8,128)}, f32[384,384]{1,0:T(8,128)}, f32[384,1536]{1,0:T(8,128)}, ...) | async-done | bytes 7077904 | tf_op jit(solution)/shard_map/psum | solution.py:303
  458.1 55.9 %all-reduce.30.cloned.1.call-done = (f32[384,384]{1,0:T(8,128)}, f32[384,384]{1,0:T(8,128)}, f32[384,384]{1,0:T(8,128)}, f32[384,384]{1,0:T(8,128)}) async-done(((f32[384,384]{1,0:T(8,128)}, f32[384,384]{1,0:T(8,128)}, f32[384,384]{1,0:T(8,128)}, f32[384,384]{1,0:T(8,128)}), (f32[384,384]{1,0:T(8,128)}, f32[384,384]{1,0:T(8,128)}, f32[384,384]{1,0:T(8,128)}, ...) | async-done | bytes 2359312 | tf_op jit(solution)/shard_map/psum | solution.py:113
  516.5 2.8 fusion.92
  534.8 2.8 fusion.75
  541.0 56.4 %all-reduce.28.cloned.1.call-done = (f32[384,384]{1,0:T(8,128)}, f32[384,384]{1,0:T(8,128)}, f32[384,384]{1,0:T(8,128)}, f32[384,384]{1,0:T(8,128)}) async-done(((f32[384,384]{1,0:T(8,128)}, f32[384,384]{1,0:T(8,128)}, f32[384,384]{1,0:T(8,128)}, f32[384,384]{1,0:T(8,128)}), (f32[384,384]{1,0:T(8,128)}, f32[384,384]{1,0:T(8,128)}, f32[384,384]{1,0:T(8,128)}, ...) | async-done | bytes 2359312 | tf_op jit(solution)/shard_map/psum | solution.py:113
  597.4 2.8 fusion.93
  617.5 9.2 %multiply_reduce_fusion.2 = (f32[384]{0:T(512)}, f32[384]{0:T(512)}, f32[384]{0:T(512)}, f32[384]{0:T(512)}, f32[384]{0:T(512)}, /*index=5*/f32[384]{0:T(512)}, f32[384]{0:T(512)}, f32[384]{0:T(512)}, f32[384]{0:T(512)}) fusion(f32[2,24,24,384]{3,2,1,0:T(8,128)S(1)} %bitcast.197, f32[2,24,24,384]{3,2,1,0:T(8,128)} %copy-done.17), kind=kLoop, calls=%fused_computation.128 | loop fusion | flops 7959168 | bytes 3552768 | tf_op jit(solution)/shard_map/reduce_sum | solution.py:78
  626.7 47.2 %all-reduce.26.cloned.1.call-done = (f32[384,384]{1,0:T(8,128)}, f32[384,384]{1,0:T(8,128)}, f32[384,384]{1,0:T(8,128)}, f32[384,384]{1,0:T(8,128)}) async-done(((f32[384,384]{1,0:T(8,128)}, f32[384,384]{1,0:T(8,128)}, f32[384,384]{1,0:T(8,128)}, f32[384,384]{1,0:T(8,128)}), (f32[384,384]{1,0:T(8,128)}, f32[384,384]{1,0:T(8,128)}, f32[384,384]{1,0:T(8,128)}, ...) | async-done | bytes 2359312 | tf_op jit(solution)/shard_map/psum | solution.py:113
  673.9 2.8 fusion.94
  697.1 2.5 convert_reduce_fusion.1
  700.0 6.0 fusion.20
  706.9 40.5 %all-reduce.4 = (f32[40,384]{1,0:T(8,128)S(1)}, f32[8]{0:T(128)S(1)}) all-reduce(f32[40,384]{1,0:T(8,128)S(1)} %concatenate.15, f32[8]{0:T(128)S(1)} %multiply_reduce_fusion.37), channel_id=1, replica_groups=mesh['wide'=8,'narrow'=4] {'wide','narrow'}, use_global_device_ids=true, to_apply=%region_66.67 | all-reduce | flops 15368 | bytes 122944 | tf_op jit(solution)/shard_map/psum | solution.py:303
  748.0 2.5 all-reduce.24.cloned.1.call-done
  750.5 2.9 fusion.95
  772.6 2.9 fusion.19
  775.5 52.1 %all-reduce.22.cloned.1.call-done = (f32[384,384]{1,0:T(8,128)}, f32[384,384]{1,0:T(8,128)}, f32[384,384]{1,0:T(8,128)}, f32[384,384]{1,0:T(8,128)}) async-done(((f32[384,384]{1,0:T(8,128)}, f32[384,384]{1,0:T(8,128)}, f32[384,384]{1,0:T(8,128)}, f32[384,384]{1,0:T(8,128)}), (f32[384,384]{1,0:T(8,128)}, f32[384,384]{1,0:T(8,128)}, f32[384,384]{1,0:T(8,128)}, ...) | async-done | bytes 2359312 | tf_op jit(solution)/shard_map/psum | solution.py:113
  827.6 2.7 fusion.96
  830.3 3.3 fusion.181
  835.0 3.3 fusion.180
  (577 shorter events, 139.8 us)
Async XLA Ops:
  7.2 9.5 %copy-start.20 = (bf16[2,576,384]{2,1,0:T(8,128)(2,1)S(1)}, bf16[2,576,384]{2,1,0:T(8,128)(2,1)}, u32[]{:S(2)}) copy-start(bf16[2,576,384]{2,1,0:T(8,128)(2,1)} %param.15) | copy-start | bytes 2654212
  7.2 8.6 %copy-start.200 = (s32[2,2]{1,0:T(2,128)S(1)}, s32[2,2]{1,0:T(2,128)}, u32[]{:S(2)}) copy-start(s32[2,2]{1,0:T(2,128)} %param.17) | copy-start | bytes 52
  7.2 435.0 %all-reduce.20.cloned.1.call-start = ((), (), s32[]{:S(2)}) async-start(), calls=%async_computation | async-start | bytes 14155776 | tf_op jit(solution)/shard_map/psum | solution.py:303
  8.9 11.1 %copy-start.161 = (f32[384]{0:T(512)}, f32[384]{0:T(512)S(1)}, u32[]{:S(2)}) copy-start(f32[384]{0:T(512)S(1)} %get-tuple-element.92) | copy-start | bytes 4612
  8.9 11.1 %copy-start.201 = (f32[384]{0:T(512)}, f32[384]{0:T(512)S(1)}, u32[]{:S(2)}) copy-start(f32[384]{0:T(512)S(1)} %get-tuple-element.91) | copy-start | bytes 4612
  8.9 29.2 %copy-start.106 = (f32[384]{0:T(512)}, f32[384]{0:T(512)S(1)}, u32[]{:S(2)}) copy-start(f32[384]{0:T(512)S(1)} %get-tuple-element.90) | copy-start | bytes 4612
  8.9 29.2 %copy-start.118 = (f32[384]{0:T(512)}, f32[384]{0:T(512)S(1)}, u32[]{:S(2)}) copy-start(f32[384]{0:T(512)S(1)} %get-tuple-element.93) | copy-start | bytes 4612
  8.9 32.1 %copy-start.95 = (f32[384]{0:T(512)}, f32[384]{0:T(512)S(1)}, u32[]{:S(2)}) copy-start(f32[384]{0:T(512)S(1)} %get-tuple-element.88) | copy-start | bytes 4612
  25.4 6.4 copy-start.5
  45.9 89.0 %copy-start = (f32[2,24,24,384]{3,2,1,0:T(8,128)}, f32[2,24,24,384]{3,2,1,0:T(8,128)S(1)}, u32[]{:S(2)}) copy-start(f32[2,24,24,384]{3,2,1,0:T(8,128)S(1)} %get-tuple-element.155) | copy-start | bytes 5308420
  209.7 12.0 %copy-start.76 = (f32[2,24,24]{2,1,0:T(8,128)S(1)}, f32[2,24,24]{2,1,0:T(8,128)}, u32[]{:S(2)}) copy-start(f32[2,24,24]{2,1,0:T(8,128)} %copy-done.74) | copy-start | bytes 13828
  209.7 12.0 %copy-start.96 = (f32[384]{0:T(512)S(1)}, f32[384]{0:T(512)}, u32[]{:S(2)}) copy-start(f32[384]{0:T(512)} %copy-done.95) | copy-start | bytes 4612
  209.7 12.0 %copy-start.123 = (f32[384]{0:T(512)S(1)}, f32[384]{0:T(512)}, u32[]{:S(2)}) copy-start(f32[384]{0:T(512)} %get-tuple-element.81) | copy-start | bytes 4612
  209.7 12.0 %copy-start.125 = (f32[384]{0:T(512)S(1)}, f32[384]{0:T(512)}, u32[]{:S(2)}) copy-start(f32[384]{0:T(512)} %get-tuple-element.82) | copy-start | bytes 4612
  209.7 12.0 %copy-start.127 = (f32[384]{0:T(512)S(1)}, f32[384]{0:T(512)}, u32[]{:S(2)}) copy-start(f32[384]{0:T(512)} %get-tuple-element.83) | copy-start | bytes 4612
  209.7 12.0 %copy-start.129 = (f32[384]{0:T(512)S(1)}, f32[384]{0:T(512)}, u32[]{:S(2)}) copy-start(f32[384]{0:T(512)} %get-tuple-element.84) | copy-start | bytes 4612
  209.8 12.0 %copy-start.131 = (f32[384]{0:T(512)S(1)}, f32[384]{0:T(512)}, u32[]{:S(2)}) copy-start(f32[384]{0:T(512)} %get-tuple-element.85) | copy-start | bytes 4612
  209.8 12.0 %copy-start.133 = (f32[384]{0:T(512)S(1)}, f32[384]{0:T(512)}, u32[]{:S(2)}) copy-start(f32[384]{0:T(512)} %get-tuple-element.86) | copy-start | bytes 4612
  209.8 12.0 %copy-start.135 = (f32[384]{0:T(512)S(1)}, f32[384]{0:T(512)}, u32[]{:S(2)}) copy-start(f32[384]{0:T(512)} %get-tuple-element.77) | copy-start | bytes 4612
  209.8 12.0 %copy-start.137 = (f32[384]{0:T(512)S(1)}, f32[384]{0:T(512)}, u32[]{:S(2)}) copy-start(f32[384]{0:T(512)} %get-tuple-element.78) | copy-start | bytes 4612
  209.8 12.0 %copy-start.139 = (f32[384]{0:T(512)S(1)}, f32[384]{0:T(512)}, u32[]{:S(2)}) copy-start(f32[384]{0:T(512)} %get-tuple-element.79) | copy-start | bytes 4612
  229.9 8.0 copy-start.119
  277.0 165.3 %copy-start.77 = (f32[384,384]{1,0:T(8,128)S(1)}, f32[384,384]{1,0:T(8,128)}, u32[]{:S(2)}) copy-start(f32[384,384]{1,0:T(8,128)} %param.26) | copy-start | bytes 1769476
  277.0 237.0 %all-reduce.30.cloned.1.call-start = ((), (), s32[]{:S(2)}) async-start(), calls=%async_computation.5 | async-start | bytes 4718592 | tf_op jit(solution)/shard_map/psum | solution.py:113
  444.3 81.1 %copy-start.36 = (f32[384,384]{1,0:T(8,128)}, f32[384,384]{1,0:T(8,128)S(1)}, u32[]{:S(2)}) copy-start(f32[384,384]{1,0:T(8,128)S(1)} %get-tuple-element.135) | copy-start | bytes 1769476
  448.4 70.9 %copy-start.37 = (f32[384,384]{1,0:T(8,128)}, f32[384,384]{1,0:T(8,128)S(1)}, u32[]{:S(2)}) copy-start(f32[384,384]{1,0:T(8,128)S(1)} %get-tuple-element.133) | copy-start | bytes 1769476
  456.1 75.3 %copy-start.73 = (f32[96,384]{1,0:T(8,128)}, f32[96,384]{1,0:T(8,128)S(1)}, u32[]{:S(2)}) copy-start(f32[96,384]{1,0:T(8,128)S(1)} %get-tuple-element.137) | copy-start | bytes 442372
  457.6 139.8 %all-reduce.28.cloned.1.call-start = ((), (), s32[]{:S(2)}) async-start(), calls=%async_computation.4 | async-start | bytes 4718592 | tf_op jit(solution)/shard_map/psum | solution.py:113
  541.0 132.9 %all-reduce.26.cloned.1.call-start = ((), (), s32[]{:S(2)}) async-start(), calls=%async_computation.3 | async-start | bytes 4718592 | tf_op jit(solution)/shard_map/psum | solution.py:113
  617.4 133.1 %all-reduce.24.cloned.1.call-start = ((), (), s32[]{:S(2)}) async-start(), calls=%async_computation.2 | async-start | bytes 4718592 | tf_op jit(solution)/shard_map/psum | solution.py:113
  626.7 50.0 %copy-start.23 = (f32[384,384]{1,0:T(8,128)S(1)}, f32[384,384]{1,0:T(8,128)}, u32[]{:S(2)}) copy-start(f32[384,384]{1,0:T(8,128)} %copy-done.22) | copy-start | bytes 1769476
  692.8 134.8 %all-reduce.22.cloned.1.call-start = ((), (), s32[]{:S(2)}) async-start(), calls=%async_computation.1 | async-start | bytes 4718592 | tf_op jit(solution)/shard_map/psum | solution.py:113
  699.8 6.4 copy-start.175
  699.8 6.4 copy-start.174
  699.8 6.4 copy-start.173
  699.8 6.4 copy-start.172
  699.8 6.4 copy-start.171
  699.9 6.4 copy-start.170
  699.9 6.4 copy-start.169
  699.9 6.4 copy-start.168
  699.9 6.4 copy-start.167
  699.9 6.5 copy-start.166
  699.9 6.5 copy-start.204
  699.9 6.5 copy-start.203
  699.9 6.5 copy-start.195
  699.9 6.7 copy-start.35
  747.4 23.7 %copy-start.206 = (f32[8]{0:T(128)}, f32[8]{0:T(128)S(1)}, u32[]{:S(2)}) copy-start(f32[8]{0:T(128)S(1)} %get-tuple-element.99) | copy-start | bytes 100
  775.5 54.8 %copy-start.29 = (f32[384,384]{1,0:T(8,128)S(1)}, f32[384,384]{1,0:T(8,128)}, u32[]{:S(2)}) copy-start(f32[384,384]{1,0:T(8,128)} %copy-done.28) | copy-start | bytes 1769476
  (165 other events, 472.5 us)
Sparse Core Ops, SparseCore 0:
  277.1 165.0 all-reduce.19
  457.8 56.2 all-reduce.29
  541.1 56.2 all-reduce.27
  617.6 56.2 all-reduce.25
  692.9 57.5 all-reduce.23
  771.3 56.2 all-reduce.21
where the time goes:
time: 857 us; the launch traced here: 852 us
  waiting for transfers between devices  379 us (44%)
  matrix products  168 us (20%)
  blocking collectives  164 us (19%)
  other arithmetic  83.8 us (10%)
  local copies, waits for them, and re-layouts  35.3 us (4%)
  between operations  20.7 us (2%)
    psum x5, waiting for transfers between devices, gram_sum(): lax.psum((local_gram(fields[0], tall_flags[0]), local_gram(fields[1], tal...  214 us
    psum x1, waiting for transfers between devices, on_device(): lax.psum((grad_wq, grad_wp, grad_w1, grad_w2, grad_vec, sharpness_adjoint...  165 us
    psum x1, blocking collectives, on_device(): lax.psum((token_sum(activated * inside_col), local_count), ('wide', 'narr...  42.3 us
    psum x1, blocking collectives, on_device(): lax.psum(token_sum(deviation * deviation), ('wide', 'narrow'))  41 us
    psum x1, blocking collectives, on_device(): lax.psum((grad_wq, grad_wp, grad_w1, grad_w2, grad_vec, sharpness_adjoint...  40.5 us
    psum x1, blocking collectives, on_device(): lax.psum((token_sum(grad_bn), token_sum(grad_bn * unit_bn)), ('wide', 'na...  40.5 us
    dot_general x20, matrix products, polish(): jnp.dot(gram_now, gram_now, precision=highest)  34.7 us
    reduce_sum x8, other arithmetic, token_sum(): return jnp.sum(source, axis=(0, 1))  21.4 us
  transfers between devices with their start and end apart: 6, of which 6 were waited for; matrix products, arithmetic and copies ran while one was open for 3% of the time, Pallas kernels for 0%

commit v1 on v0

--- a/solution.py
+++ b/solution.py
@@ -103,31 +103,90 @@
     return jnp.einsum("gsk,gse->ke", left, right, preferred_element_type=jnp.float32)
 
 
-def local_gram(source, is_tall):
-    if is_tall:
-        return jnp.dot(source.T, source, precision=highest)
-    return jnp.dot(source, source.T, precision=highest)
-
-
-def gram_sum(fields, tall_flags):
-    return lax.psum(
-        (
-            local_gram(fields[0], tall_flags[0]),
-            local_gram(fields[1], tall_flags[1]),
-            local_gram(fields[2], tall_flags[2]),
-            local_gram(fields[3], tall_flags[3]),
-        ),
-        "narrow",
-    )
-
-
-def polish(source, gram_now, is_tall):
-    polynomial = coef_second * gram_now + coef_third * jnp.dot(
-        gram_now, gram_now, precision=highest
-    )
-    if is_tall:
-        return coef_first * source + jnp.dot(source, polynomial, precision=highest)
-    return coef_first * source + jnp.dot(polynomial, source, precision=highest)
+def fold_bits(size):
+    return [1 << place for place in range(size.bit_length() - 1)]
+
+
+def swap(source, axis, bit):
+    size = lax.axis_size(axis)
+    return lax.ppermute(source, axis, [(member, member ^ bit) for member in range(size)])
+
+
+def everyone(rows):
+    devices = lax.axis_size("wide") * lax.axis_size("narrow")
+    copies = jnp.broadcast_to(rows[None], (devices,) + rows.shape)
+    return lax.all_to_all(copies, ("wide", "narrow"), 0, 0, tiled=True)
+
+
+def pick(source, index):
+    return lax.dynamic_index_in_dim(source, index, 0, keepdims=False)
+
+
+def scatter_sum(bundle):
+    narrow_pos = lax.axis_index("narrow")
+    wide_pos = lax.axis_index("wide")
+    held = bundle
+    for bit in fold_bits(lax.axis_size("narrow")):
+        mine = (narrow_pos // bit) % 2
+        pairs = held.reshape((held.shape[0] // 2, 2) + held.shape[1:]).swapaxes(0, 1)
+        held = pick(pairs, mine) + swap(pick(pairs, 1 - mine), "narrow", bit)
+    held = held[0]
+    for bit in fold_bits(lax.axis_size("wide")):
+        mine = (wide_pos // bit) % 2
+        halves = held.reshape((2, held.shape[0] // 2) + held.shape[1:])
+        held = pick(halves, mine) + swap(pick(halves, 1 - mine), "wide", bit)
+    return held
+
+
+def gather_wide(share):
+    wide_pos = lax.axis_index("wide")
+    held = share
+    for bit in reversed(fold_bits(lax.axis_size("wide"))):
+        other = swap(held, "wide", bit)
+        low = (wide_pos // bit) % 2 == 0
+        held = jnp.concatenate([jnp.where(low, held, other), jnp.where(low, other, held)])
+    return held
+
+
+def gather_narrow(share):
+    narrow_pos = lax.axis_index("narrow")
+    held = share[None]
+    for bit in reversed(fold_bits(lax.axis_size("narrow"))):
+        other = swap(held, "narrow", bit)
+        low = (narrow_pos // bit) % 2 == 0
+        held = jnp.stack([jnp.where(low, held, other), jnp.where(low, other, held)], axis=1)
+        held = held.reshape((-1,) + share.shape)
+    return held
+
+
+def dot3(left, right):
+    return jnp.dot(left, right, precision=lax.Precision.HIGH)
+
+
+def polynomial_of(gram):
+    norm = jnp.sqrt(jnp.trace(gram)) + frob_eps
+    now = gram / (norm * norm)
+    identity = jnp.eye(gram.shape[0], dtype=jnp.float32)
+    total = None
+    for sweep_index in range(NS_STEPS):
+        step = coef_first * identity + coef_second * now + coef_third * dot3(now, now)
+        total = step / norm if total is None else dot3(step, total)
+        if sweep_index < NS_STEPS - 1:
+            now = dot3(dot3(step, now), step)
+    return total
+
+
+def orthogonal_pair(first, second, grams):
+    narrow_pos = lax.axis_index("narrow")
+    even = narrow_pos % 2 == 0
+    mine = jnp.where(even, grams[0], grams[1]) + swap(
+        jnp.where(even, grams[1], grams[0]), "narrow", 1
+    )
+    for bit in fold_bits(lax.axis_size("narrow"))[1:]:
+        mine = mine + swap(mine, "narrow", bit)
+    result = polynomial_of(mine)
+    other = swap(result, "narrow", 1)
+    return first(jnp.where(even, result, other)), second(jnp.where(even, other, result))
 
 
 def on_device(
@@ -192,11 +251,20 @@
     conv_one = depthwise(local_in, affine_entries[9:18]).reshape(flat_shape) + affine_entries[18]
     activated = gelu_exact(conv_one)
     local_count = jnp.sum(interior_patches)
-    first_sums = lax.psum((token_sum(activated * inside_col), local_count), ("wide", "narrow"))
-    genuine_patch_tally = first_sums[1]
-    centre_mean = first_sums[0] / genuine_patch_tally
-    deviation = (activated - centre_mean) * inside_col
-    variance = lax.psum(token_sum(deviation * deviation), ("wide", "narrow")) / genuine_patch_tally
+    local_sum = token_sum(activated * inside_col)
+    local_mean = local_sum / local_count
+    local_dev = (activated - local_mean) * inside_col
+    first_rows = jnp.stack(
+        [local_sum, token_sum(local_dev * local_dev), jnp.full_like(local_sum, local_count)]
+    )
+    first_all = everyone(first_rows)
+    counts = first_all[:, 2]
+    genuine_patch_tally = jnp.sum(counts[:, 0])
+    centre_mean = jnp.sum(first_all[:, 0], axis=0) / genuine_patch_tally
+    shifts = first_all[:, 0] / counts - centre_mean
+    variance = (
+        jnp.sum(first_all[:, 1] + counts * shifts * shifts, axis=0) / genuine_patch_tally
+    )
     inverse_std = lax.rsqrt(variance + batch_eps)
     unit_bn = (activated - centre_mean) * inverse_std * inside_col
     normal_bn = (unit_bn * affine_entries[19] + affine_entries[20]) * inside_col
@@ -220,7 +288,7 @@
     grad_w2 = outer_sum(hidden_low, grad_branch3)
     grad_hidden = (right_mul_t(grad_branch3, two_low) * gelu_slope(hidden)).astype(jnp.bfloat16)
     bias_fc1 = token_sum(grad_hidden.astype(jnp.float32)).reshape(4, model_width)
-    grad_w1 = outer_sum(norm_three_low, grad_hidden)
+    grad_w1 = outer_sum(grad_hidden, norm_three_low)
     grad_norm3 = right_mul_t(grad_hidden, one_low)
     gain_three = token_sum(grad_norm3 * unit_three)
     shift_three = token_sum(grad_norm3)
@@ -231,7 +299,9 @@
     grad_conv2_grid = grad_conv2.reshape(grid_shape)
     kernel_two = kernel_grad(normal_grid, grad_conv2_grid)
     grad_bn = depthwise(grad_conv2_grid, affine_entries[29:20:-1]).reshape(flat_shape) * inside_col
-    bn_grads = lax.psum((token_sum(grad_bn), token_sum(grad_bn * unit_bn)), ("wide", "narrow"))
+    bn_grads = jnp.sum(
+        everyone(jnp.stack([token_sum(grad_bn), token_sum(grad_bn * unit_bn)])), axis=0
+    )
     bias_bn = bn_grads[0]
     gain_bn = bn_grads[1]
     grad_act = (
@@ -274,7 +344,7 @@
     grad_key = unit_back(grad_kunit, key_unit, key_inv) * inside_col
     grad_joined = jnp.concatenate([grad_query, grad_key, grad_value], axis=-1).astype(jnp.bfloat16)
     bias_qkv = token_sum(grad_joined.astype(jnp.float32)).reshape(3, model_width)
-    grad_wq = outer_sum(norm_one_low, grad_joined)
+    grad_wq = outer_sum(grad_joined, norm_one_low)
     grad_norm1 = right_mul_t(grad_joined, asker_lowprec)
     gain_one = token_sum(grad_norm1 * unit_one)
     shift_one = token_sum(grad_norm1)
@@ -300,40 +370,44 @@
         part_size = full_matrix.shape[along] // narrow_parts
         return lax.dynamic_slice_in_dim(full_matrix, narrow_pos * part_size, part_size, along)
 
-    summed = lax.psum(
-        (grad_wq, grad_wp, grad_w1, grad_w2, grad_vec, sharpness_adjoint), ("wide", "narrow")
-    )
-    shard_grads = (
-        own_part(summed[0], 1),
-        own_part(summed[1], 0),
-        own_part(summed[2], 1),
-        own_part(summed[3], 0),
-    )
-    vec_total = summed[4]
-    sharpness_sum = summed[5]
+    def parts_of(full_matrix):
+        return full_matrix.reshape((narrow_parts, -1) + full_matrix.shape[1:])
+
+    fed_bundle = jnp.concatenate([parts_of(grad_w1), parts_of(grad_w2)], axis=1)
+    fed_rows = grad_w1.shape[0] // narrow_parts
+    fed_share = gather_wide(scatter_sum(fed_bundle))
+    shard_w1 = fed_share[:fed_rows].T
+    shard_w2 = fed_share[fed_rows:]
+
+    vec_rows = jnp.zeros((narrow_parts * 64, model_width), jnp.float32)
+    vec_rows = vec_rows.at[: grad_vec.shape[0]].set(grad_vec)
+    vec_rows = vec_rows.at[grad_vec.shape[0], :group_index].set(sharpness_adjoint)
+    att_bundle = jnp.concatenate(
+        [parts_of(grad_wq), parts_of(grad_wp), parts_of(vec_rows)], axis=1
+    )
+    att_rows = grad_wq.shape[0] // narrow_parts
+    mix_rows = grad_wp.shape[0] // narrow_parts
+    att_share = gather_wide(scatter_sum(att_bundle))
+    shard_wq = att_share[:att_rows].T
+    shard_wp = att_share[att_rows : att_rows + mix_rows]
+    vec_share = gather_narrow(att_share[att_rows + mix_rows :]).reshape(-1, model_width)
+    vec_total = vec_share[: grad_vec.shape[0]]
+    sharpness_sum = vec_share[grad_vec.shape[0], :group_index]
+    shard_grads = (shard_wq, shard_wp, shard_w1, shard_w2)
     vec_full = jnp.concatenate([vec_total[:19], jnp.stack([gain_bn, bias_bn]), vec_total[21:]])
-    tall_flags = (
-        triple_matrix.shape[0] >= triple_matrix.shape[1],
-        mixer_matrix.shape[0] >= mixer_matrix.shape[1],
-        expand_matrix.shape[0] >= expand_matrix.shape[1],
-        shrink_matrix.shape[0] >= shrink_matrix.shape[1],
-    )
     moments = (triple_velocity, mixer_velocity, expand_velocity, shrink_velocity)
     states = [velocity_damping * moments[member] + shard_grads[member] for member in range(4)]
-
-    def gram_list(fields):
-        return gram_sum(fields, tall_flags)
-
-    raw_grams = gram_list(states)
-    norms = [jnp.sqrt(jnp.trace(raw_grams[member])) + frob_eps for member in range(4)]
-    fields = [states[member] / norms[member] for member in range(4)]
-    gram_set = [raw_grams[member] / (norms[member] * norms[member]) for member in range(4)]
-    for sweep_index in range(NS_STEPS):
-        if sweep_index > 0:
-            gram_set = gram_list(fields)
-        fields = [
-            polish(fields[member], gram_set[member], tall_flags[member]) for member in range(4)
-        ]
+    fed_fields = orthogonal_pair(
+        lambda poly: dot3(poly, states[2]),
+        lambda poly: dot3(states[3], poly),
+        (dot3(states[2], states[2].T), dot3(states[3].T, states[3])),
+    )
+    att_fields = orthogonal_pair(
+        lambda poly: dot3(poly, states[0]),
+        lambda poly: dot3(states[1], poly),
+        (dot3(states[0], states[0].T), dot3(states[1].T, states[1])),
+    )
+    fields = att_fields + fed_fields
     full_weights = (triple_matrix, mixer_matrix, expand_matrix, shrink_matrix)
     factors = [
         math.sqrt(max(1.0, full_weights[member].shape[0] / full_weights[member].shape[1]))

time: 857 us -> 377 us (0.44)
  waiting for transfers between devices: 379 us -> 90.4 us
  blocking collectives: 164 us -> 0 us
  matrix products: 168 us -> 98.4 us
  starting transfers between devices: 0.65 us -> 40.9 us
  local copies, waits for them, and re-layouts: 35.3 us -> 50.8 us
  between operations: 20.7 us -> 5.85 us
    psum x6 -> x0, waiting for transfers between devices: 379 us -> none  [the longest x5 214 us: gram_sum(): lax.psum((local_gram(fields[0], tall_flags[0]), local_gram(fields[1], tal...]
    psum x4 -> x0, blocking collectives: 164 us -> none  [the longest x1 42.3 us: on_device(): lax.psum((token_sum(activated * inside_col), local_count), ('wide', 'narr...]
    ppermute x0 -> x24, waiting for transfers between devices: none -> 84.2 us  [swap(): lax.ppermute(source, axis, [(member, member ^ bit) for member in range(si...]
    dot_general x60 -> x42, matrix products: 102 us -> 37.7 us  [dot3(): return jnp.dot(left, right, precision=lax.Precision.HIGH)]
    ppermute x0 -> x24, starting transfers between devices: none -> 29.6 us  [swap(): lax.ppermute(source, axis, [(member, member ^ bit) for member in range(si...]
    all_to_all x0 -> x2, starting transfers between devices: none -> 11.4 us  [everyone(): return lax.all_to_all(copies, ('wide', 'narrow'), 0, 0, tiled=True)]
  transfers between devices with their start and end apart: 6 -> 26, of which waited for: 6 -> 18; matrix products, arithmetic and copies ran while one was open for 3% -> 21% of each run, Pallas kernels for 0% -> 0%
where the time goes in v1:
time: 377 us; the launch traced here: 371 us
  matrix products  98.4 us (26%)
  waiting for transfers between devices  90.4 us (24%)
  other arithmetic  84.5 us (22%)
  local copies, waits for them, and re-layouts  50.8 us (13%)
  starting transfers between devices  40.9 us (11%)
  between operations  5.85 us (2%)
    ppermute x24, waiting for transfers between devices, swap(): lax.ppermute(source, axis, [(member, member ^ bit) for member in range(si...  84.2 us
    dot_general x42, matrix products, dot3(): return jnp.dot(left, right, precision=lax.Precision.HIGH)  37.7 us
    ppermute x24, starting transfers between devices, swap(): lax.ppermute(source, axis, [(member, member ^ bit) for member in range(si...  29.6 us
    reduce_sum x2, other arithmetic, kernel_grad(): jnp.sum(padded[:, offset // 3:offset // 3 + grid_side, offset % 3:offset...  21.1 us
    dot_general x4, matrix products, right_mul(): jnp.einsum('gsk,ke->gse', left, right, preferred_element_type=jnp.float32)  17.8 us
    reduce_sum x8, other arithmetic, token_sum(): return jnp.sum(source, axis=(0, 1))  15.3 us
    dot_general x4, matrix products, right_mul_t(): jnp.einsum('gse,ke->gsk', left, right, preferred_element_type=jnp.float32)  13.1 us
    dot_general x4, matrix products, outer_sum(): jnp.einsum('gsk,gse->ke', left, right, preferred_element_type=jnp.float32)  11.9 us
  transfers between devices with their start and end apart: 26, of which 18 were waited for; matrix products, arithmetic and copies ran while one was open for 21% of the time, Pallas kernels for 0%

profile of v1, /device:TPU:0, one launch (start us, length us, event | category | flops | bytes accessed | tf_op | source)
XLA Modules:
  0.0 370.9 jit_solution(3399157483484876594)
XLA Ops:
  9.8 3.2 convolution_add_fusion
  13.5 2.3 fusion.79
  19.8 3.6 copy.105
  23.4 4.0 %multiply_reduce_fusion.39 = (f32[2,8,48]{2,1,0:T(8,128)S(1)}, f32[2,8,48,48]{2,3,1,0:T(8,128)S(1)}) fusion(f32[8]{0:T(128)S(1)} %copy-done.69, f32[2,576,8,48]{1,3,2,0:T(8,128)S(1)} %bitcast.251, f32[2,576,8,48]{1,3,2,0:T(8,128)} %bitcast.253), kind=kOutput, calls=%fused_computation.285 | convolution fusion | flops 254876928 | bytes 3689504 | tf_op jit(solution)/shard_map/gshi,gshj->ghij/dot_general | solution.py:240
  33.2 2.7 multiply_reduce_fusion.30
  38.7 7.9 %all-to-all-start = ((f32[32,3,384]{2,1,0:T(4,128)}), f32[32,3,384]{2,1,0:T(4,128)}, u32[]{:S(2)}, u32[]{:S(2)}) async-start(f32[32,3,384]{2,1,0:T(4,128)} %broadcast_in_dim.8), calls=%async_computation | async-start | bytes 393216 | tf_op jit(solution)/shard_map/all_to_all | solution.py:118
  49.2 6.3 %all-to-all-done = f32[32,3,384]{2,1,0:T(4,128)} async-done(((f32[32,3,384]{2,1,0:T(4,128)}), f32[32,3,384]{2,1,0:T(4,128)}, u32[]{:S(2)}, u32[]{:S(2)}) %all-to-all-start) | async-done | bytes 147488 | tf_op jit(solution)/shard_map/all_to_all | solution.py:118
  65.7 4.3 %multiply_convert_fusion = (bf16[2,576,1536]{2,1,0:T(8,128)(2,1)}, f32[2,576,1536]{2,1,0:T(8,128)S(1)}) fusion(f32[1536]{0:T(1024)S(1)} %copy-done.141, f32[384,1536]{1,0:T(8,128)S(1)} %copy-done.56, f32[2,576,384]{2,1,0:T(8,128)S(1)} %get-tuple-element.248, f32[384]{0:T(512)S(1)} %copy-done.159, f32[384]{0:T(512)S(1)} %copy-done.119, ...), kind=kOutput, calls=%fused_computation.10 | convolution fusion | flops 1372372992 | bytes 14764032 | tf_op jit(solution)/shard_map/gsk,ke->gse/dot_general | solution.py:95
  70.1 5.4 %convert_reduce_fusion = (f32[1536]{0:T(1024)}, bf16[2,576,1536]{2,1,0:T(8,128)(2,1)S(1)}) fusion(f32[2,576,1536]{2,1,0:T(8,128)S(1)} %get-tuple-element.286, f32[1536]{0:T(1024)S(1)} %copy-done.141, f32[1536,384]{1,0:T(8,128)S(1)} %copy-done.29, bf16[2,576,384]{2,1,0:T(8,128)(2,1)S(1)} %copy-done.31, f32[384]{0:T(512)S(1)} %copy-done.84, ...), kind=kOutput, calls=%fused_computation.9 | convolution fusion | flops 1384315392 | bytes 13879296 | tf_op jit(solution)/shard_map/gse,ke->gsk/dot_general | solution.py:99
  75.4 3.0 multiply_reduce_fusion
  78.5 2.5 fusion.171
  81.0 3.6 fusion.169
  85.3 3.5 all-to-all-start.1
  88.8 8.7 %multiply_reduce_fusion.2 = (f32[384]{0:T(512)S(1)}, f32[384]{0:T(512)S(1)}, f32[384]{0:T(512)S(1)}, f32[384]{0:T(512)S(1)}, f32[384]{0:T(512)S(1)}, /*index=5*/...) fusion(f32[2,24,24,384]{3,2,1,0:T(8,128)} %bitcast.262, f32[2,24,24,384]{3,2,1,0:T(8,128)} %copy-done.17), kind=kLoop, calls=%fused_computation.145 | loop fusion | flops 7959168 | bytes 3552768 | tf_op jit(solution)/shard_map/reduce_sum | solution.py:78
  108.5 12.3 %multiply_reduce_fusion.11 = (f32[384]{0:T(512)}, f32[384]{0:T(512)}, f32[384]{0:T(512)}, f32[384]{0:T(512)}, f32[384]{0:T(512)}, /*index=5*/f32[384]{0:T(512)},...) fusion(f32[2,24,24,384]{3,2,1,0:T(8,128)} %bitcast.260, ...), kind=kLoop, calls=%fused_computation.154 | loop fusion | flops 16806144 | bytes 8875012 | tf_op jit(solution)/shard_map/reduce_sum | solution.py:78
  120.9 3.2 multiply_reduce_fusion.34
  129.0 8.0 %fusion.33 = (f32[384]{0:T(512)}, f32[384]{0:T(512)}, f32[384]{0:T(512)}, f32[384]{0:T(512)}, f32[2,576,384]{2,1,0:T(8,128)S(1)}, /*index=5*/bf16[2,576,384]{2,1,0:T(8,128)(2,1)}) fusion(bf16[2,576,384]{2,1,0:T(8,128)(2,1)} %param.20, f32[384]{0:T(512)} %get-tuple-element.200, f32[2,576]{1,0:T(2,128)S(1)} %get-tuple-element.250, ...), kind=kOutput, calls=%fused_computation.99 | convolution fusion | flops 1371929088 | bytes 20089344 | tf_op jit(solution)/shard_map/gsk,ke->gse/dot_general | solution.py:95
  139.3 2.9 convolution_convert_fusion
  142.2 2.3 multiply_reduce_fusion.38
  144.5 3.3 fusion.128
  147.8 3.4 fusion.130
  151.3 2.2 copy.118
  153.4 2.8 copy.117
  156.2 4.5 %multiply_convert_fusion.1 = bf16[2,576,384]{2,1,0:T(8,128)(2,1)} fusion(f32[2,576,384]{2,1,0:T(8,128)} %copy.117, f32[2,576,384]{2,1,0:T(8,128)} %get-tuple-element.256, f32[2,384]{1,0:T(2,128)S(1)} %copy-done.77, f32[2,576]{1,0:T(2,128)S(1)} %get-tuple-element.250), kind=kOutput, calls=%fused_computation.166 | output fusion | flops 2655551 | bytes 4431360 | tf_op jit(solution)/shard_map/mul | solution.py:91
  160.7 2.8 copy.115
  163.6 3.7 %multiply_convert_fusion.2 = bf16[2,576,384]{2,1,0:T(8,128)(2,1)S(1)} fusion(f32[2,576,384]{2,1,0:T(8,128)} %copy.115, f32[2,576,384]{2,1,0:T(8,128)} %get-tuple-element.257, f32[2,384]{1,0:T(2,128)S(1)} %copy-done.75, f32[2,576]{1,0:T(2,128)S(1)} %get-tuple-element.250), kind=kOutput, calls=%fused_computation.169 | output fusion | flops 2655551 | bytes 4431360 | tf_op jit(solution)/shard_map/mul | solution.py:91
  167.9 4.1 %fusion.25 = (f32[384]{0:T(512)S(1)}, f32[2,576]{1,0:T(2,128)}, f32[2,576]{1,0:T(2,128)}, f32[384]{0:T(512)S(1)}, f32[2,576,384]{2,1,0:T(8,128)}) fusion(bf16[2,576,384]{2,1,0:T(8,128)(2,1)S(1)} %copy-done.19, f32[2,576]{1,0:T(2,128)S(1)} %copy-done.82, f32[2,576]{1,0:T(2,128)S(1)} %copy-done.67, f32[384]{0:T(512)S(1)} %copy-done.117, ...), kind=kOutput, calls=%fused_computation.91 | convolution fusion | flops 1032041472 | bytes 7100928 | tf_op jit(solution)/shard_map/gse,ke->gsk/dot_general | solution.py:99
  173.5 3.1 fusion.122
  183.5 2.9 collective-permute-done
  191.0 4.4 %fusion.154 = f32[1536,384,1]{1,0,2:T(8,128)S(1)} fusion(bf16[2,576,1536]{2,1,0:T(8,128)(2,1)} %copy-done.166, f32[2,576,384]{2,1,0:T(8,128)S(1)} %copy-done.3, f32[384]{0:T(512)S(1)} %copy-done.160, f32[384]{0:T(512)S(1)} %copy-done.120, f32[2,576]{1,0:T(2,128)S(1)} %copy-done.80, f32[2,576]{1,0:T(2,128)S(1)} %copy-done.65), kind=kOutput, calls=%fused_computation.353 | convolution fusion | flops 1361166336 | bytes 7680000 | tf_op jit(solution)/shard_map/gsk,gse->ke/dot_general | solution.py:103
  195.4 11.8 %collective-permute-done.1 = f32[1,448,384]{2,1,0:T(8,128)} collective-permute-done((f32[1,448,384]{2,1,0:T(8,128)}, f32[1,448,384]{2,1,0:T(8,128)}, u32[]{:S(2)}, u32[]{:S(2)}) %collective-permute-start.1) | collective-permute-done | bytes 688160 | tf_op jit(solution)/shard_map/ppermute | solution.py:112
  210.0 2.3 fusion.119
  214.4 3.5 collective-permute-done.2
  226.1 2.6 collective-permute-start.4
  228.6 3.8 %collective-permute-done.4 = f32[56,384]{1,0:T(8,128)S(1)} collective-permute-done((f32[56,384]{1,0:T(8,128)S(1)}, f32[56,384]{1,0:T(8,128)S(1)}, u32[]{:S(2)}, u32[]{:S(2)}) %collective-permute-start.4) | collective-permute-done | bytes 86048 | tf_op jit(solution)/shard_map/ppermute | solution.py:112
  234.2 3.8 %collective-permute-done.5 = f32[56,384]{1,0:T(8,128)S(1)} collective-permute-done((f32[56,384]{1,0:T(8,128)S(1)}, f32[56,384]{1,0:T(8,128)S(1)}, u32[]{:S(2)}, u32[]{:S(2)}) %collective-permute-start.5) | collective-permute-done | bytes 86048 | tf_op jit(solution)/shard_map/ppermute | solution.py:112
  238.1 3.4 collective-permute-start.6
  241.4 3.2 fusion.24
  256.1 15.6 %collective-permute-done.9 = f32[1,768,384]{2,1,0:T(8,128)S(1)} collective-permute-done((f32[1,768,384]{2,1,0:T(8,128)S(1)}, f32[1,768,384]{2,1,0:T(8,128)S(1)}, u32[]{:S(2)}, u32[]{:S(2)}) %collective-permute-start.9) | collective-permute-done | bytes 1179680 | tf_op jit(solution)/shard_map/ppermute | solution.py:112
  274.5 7.5 %collective-permute-done.10 = f32[384,384]{1,0:T(8,128)S(1)} collective-permute-done((f32[384,384]{1,0:T(8,128)S(1)}, f32[384,384]{1,0:T(8,128)S(1)}, u32[]{:S(2)}, u32[]{:S(2)}) %collective-permute-start.10) | collective-permute-done | bytes 589856 | tf_op jit(solution)/shard_map/ppermute | solution.py:112
  284.9 4.6 %collective-permute-done.11 = f32[192,384]{1,0:T(8,128)S(1)} collective-permute-done((f32[192,384]{1,0:T(8,128)S(1)}, f32[192,384]{1,0:T(8,128)S(1)}, u32[]{:S(2)}, u32[]{:S(2)}) %collective-permute-start.11) | collective-permute-done | bytes 294944 | tf_op jit(solution)/shard_map/ppermute | solution.py:112
  289.5 2.3 collective-permute-start.12
  292.5 4.8 %collective-permute-done.12 = f32[96,384]{1,0:T(8,128)S(1)} collective-permute-done((f32[96,384]{1,0:T(8,128)S(1)}, f32[96,384]{1,0:T(8,128)S(1)}, u32[]{:S(2)}, u32[]{:S(2)}) %collective-permute-start.12) | collective-permute-done | bytes 147488 | tf_op jit(solution)/shard_map/ppermute | solution.py:112
  308.4 3.5 collective-permute-done.14
  315.5 6.4 %collective-permute-done.15 = f32[384,384]{1,0:T(8,128)S(1)} collective-permute-done((f32[384,384]{1,0:T(8,128)S(1)}, f32[384,384]{1,0:T(8,128)S(1)}, u32[]{:S(2)}, u32[]{:S(2)}) %collective-permute-start.15) | collective-permute-done | bytes 589856 | tf_op jit(solution)/shard_map/ppermute | solution.py:112
  331.1 11.8 %collective-permute-done.22 = f32[384,384]{1,0:T(8,128)S(1)} collective-permute-done((f32[384,384]{1,0:T(8,128)S(1)}, f32[384,384]{1,0:T(8,128)S(1)}, u32[]{:S(2)}, u32[]{:S(2)}) %collective-permute-start.22) | collective-permute-done | bytes 589856 | tf_op jit(solution)/shard_map/ppermute | solution.py:112
  364.9 2.7 fusion.184
  367.6 2.9 fusion.185
  (565 shorter events, 141.9 us)
Async XLA Ops:
  2.3 27.3 %copy-start.72 = (f32[384]{0:T(512)}, f32[384]{0:T(512)S(1)}, u32[]{:S(2)}) copy-start(f32[384]{0:T(512)S(1)} %get-tuple-element.210) | copy-start | bytes 4612
  2.3 27.3 %copy-start.86 = (f32[384]{0:T(512)}, f32[384]{0:T(512)S(1)}, u32[]{:S(2)}) copy-start(f32[384]{0:T(512)S(1)} %get-tuple-element.213) | copy-start | bytes 4612
  2.3 30.1 %copy-start.60 = (f32[384]{0:T(512)}, f32[384]{0:T(512)S(1)}, u32[]{:S(2)}) copy-start(f32[384]{0:T(512)S(1)} %get-tuple-element.208) | copy-start | bytes 4612
  38.7 16.8 %all-to-all-start = ((f32[32,3,384]{2,1,0:T(4,128)}), f32[32,3,384]{2,1,0:T(4,128)}, u32[]{:S(2)}, u32[]{:S(2)}) async-start(f32[32,3,384]{2,1,0:T(4,128)} %broadcast_in_dim.8), calls=%async_computation | async-start | bytes 393216 | tf_op jit(solution)/shard_map/all_to_all | solution.py:118
  58.0 23.0 %copy-start.63 = (f32[384]{0:T(512)}, f32[384]{0:T(512)S(1)}, u32[]{:S(2)}) copy-start(f32[384]{0:T(512)S(1)} %broadcast_divide_fusion.6) | copy-start | bytes 4612
  58.7 22.3 %copy-start.73 = (f32[384]{0:T(512)}, f32[384]{0:T(512)S(1)}, u32[]{:S(2)}) copy-start(f32[384]{0:T(512)S(1)} %add_rsqrt_fusion.5) | copy-start | bytes 4612
  64.4 14.0 %copy-start.2 = (f32[2,576,384]{2,1,0:T(8,128)}, f32[2,576,384]{2,1,0:T(8,128)S(1)}, u32[]{:S(2)}) copy-start(f32[2,576,384]{2,1,0:T(8,128)S(1)} %get-tuple-element.248) | copy-start | bytes 5308420
  64.5 14.0 %copy-start.64 = (f32[2,576]{1,0:T(2,128)}, f32[2,576]{1,0:T(2,128)S(1)}, u32[]{:S(2)}) copy-start(f32[2,576]{1,0:T(2,128)S(1)} %broadcast_multiply_fusion.6) | copy-start | bytes 13828
  85.3 20.2 %all-to-all-start.1 = ((f32[32,2,384]{2,1,0:T(2,128)}), f32[32,2,384]{2,1,0:T(2,128)}, u32[]{:S(2)}, u32[]{:S(2)}) async-start(f32[32,2,384]{2,1,0:T(2,128)} %broadcast_in_dim.9), calls=%async_computation.1 | async-start | bytes 196608 | tf_op jit(solution)/shard_map/all_to_all | solution.py:118
  88.8 13.8 %copy-start.139 = (f32[384]{0:T(512)S(1)}, f32[384]{0:T(512)}, u32[]{:S(2)}) copy-start(f32[384]{0:T(512)} %get-tuple-element.238) | copy-start | bytes 4612
  88.8 14.3 %copy-start.164 = (f32[384]{0:T(512)S(1)}, f32[384]{0:T(512)}, u32[]{:S(2)}) copy-start(f32[384]{0:T(512)} %get-tuple-element.146) | copy-start | bytes 4612
  88.8 14.9 %copy-start.163 = (f32[384]{0:T(512)S(1)}, f32[384]{0:T(512)}, u32[]{:S(2)}) copy-start(f32[384]{0:T(512)} %get-tuple-element.174) | copy-start | bytes 4612
  183.1 3.3 collective-permute-start
  189.2 18.0 %collective-permute-start.1 = (f32[1,448,384]{2,1,0:T(8,128)}, f32[1,448,384]{2,1,0:T(8,128)}, u32[]{:S(2)}, u32[]{:S(2)}) collective-permute-start(f32[1,448,384]{2,1,0:T(8,128)} %constant_dynamic-slice_fusion.2), channel_id=1, source_target_pairs={{0,2},{1,3},{2,0},{3,1},{4,6},{5,7},{6,4},{7,5},{8,10},{9,11},{10,... | collective-permute-start | bytes 2064392 | tf_op jit(solution)/shard_map/ppermute | solution.py:112
  191.0 19.1 %copy-start.30 = (bf16[2,576,1536]{2,1,0:T(8,128)(2,1)S(1)}, bf16[2,576,1536]{2,1,0:T(8,128)(2,1)}, u32[]{:S(2)}) copy-start(bf16[2,576,1536]{2,1,0:T(8,128)(2,1)} %get-tuple-element.285) | copy-start | bytes 10616836
  195.4 16.9 %copy-start.22 = (f32[1536,384,1]{1,0,2:T(8,128)}, f32[1536,384,1]{1,0,2:T(8,128)S(1)}, u32[]{:S(2)}) copy-start(f32[1536,384,1]{1,0,2:T(8,128)S(1)} %fusion.154) | copy-start | bytes 7077892
  195.4 14.6 %copy-start.32 = (bf16[2,576,384]{2,1,0:T(8,128)(2,1)S(1)}, bf16[2,576,384]{2,1,0:T(8,128)(2,1)}, u32[]{:S(2)}) copy-start(bf16[2,576,384]{2,1,0:T(8,128)(2,1)} %param.20) | copy-start | bytes 2654212
  195.4 14.6 %copy-start.85 = (f32[384]{0:T(512)S(1)}, f32[384]{0:T(512)}, u32[]{:S(2)}) copy-start(f32[384]{0:T(512)} %get-tuple-element.181) | copy-start | bytes 4612
  208.4 9.6 %collective-permute-start.2 = (f32[224,384]{1,0:T(8,128)S(1)}, f32[224,384]{1,0:T(8,128)S(1)}, u32[]{:S(2)}, u32[]{:S(2)}) collective-permute-start(f32[224,384]{1,0:T(8,128)S(1)} %dynamic-slice_bitcast_fusion.2), channel_id=1, source_target_pairs={{0,4},{4,0},{8,12},{12,8},{16,20},{20,16},{24,28},{28,24},{1,5},{5... | collective-permute-start | bytes 1032200 | tf_op jit(solution)/shard_map/ppermute | solution.py:112
  214.4 32.0 %collective-permute-start.8 = (f32[2,768,384]{2,1,0:T(8,128)}, f32[2,768,384]{2,1,0:T(8,128)}, u32[]{:S(2)}, u32[]{:S(2)}) collective-permute-start(f32[2,768,384]{2,1,0:T(8,128)} %fusion.9), channel_id=1, source_target_pairs={{0,1},{1,0},{2,3},{3,2},{4,5},{5,4},{6,7},{7,6},{8,9},{9,8},{10,11... | collective-permute-start | bytes 7077896 | tf_op jit(solution)/shard_map/ppermute | solution.py:112
  219.4 5.7 %collective-permute-start.3 = (f32[112,384]{1,0:T(8,128)}, f32[112,384]{1,0:T(8,128)S(1)}, u32[]{:S(2)}, u32[]{:S(2)}) collective-permute-start(f32[112,384]{1,0:T(8,128)} %dynamic-slice_bitcast_fusion.4), channel_id=1, source_target_pairs={{0,8},{4,12},{8,0},{12,4},{16,24},{20,28},{24,16},{28,20},{1,9},{5... | collective-permute-start | bytes 516104 | tf_op jit(solution)/shard_map/ppermute | solution.py:112
  221.9 19.5 %copy-start.12 = (f32[2,576,384]{2,1,0:T(8,128)S(1)}, f32[2,576,384]{2,1,0:T(8,128)}, u32[]{:S(2)}) copy-start(f32[2,576,384]{2,1,0:T(8,128)} %copy-done.11) | copy-start | bytes 5308420
  221.9 19.5 %copy-start.20 = (bf16[2,576,384]{2,1,0:T(8,128)(2,1)S(1)}, bf16[2,576,384]{2,1,0:T(8,128)(2,1)}, u32[]{:S(2)}) copy-start(bf16[2,576,384]{2,1,0:T(8,128)(2,1)} %param.19) | copy-start | bytes 2654212
  221.9 19.5 %copy-start.68 = (f32[2,576]{1,0:T(2,128)S(1)}, f32[2,576]{1,0:T(2,128)}, u32[]{:S(2)}) copy-start(f32[2,576]{1,0:T(2,128)} %copy-done.66) | copy-start | bytes 13828
  221.9 19.5 %copy-start.83 = (f32[2,576]{1,0:T(2,128)S(1)}, f32[2,576]{1,0:T(2,128)}, u32[]{:S(2)}) copy-start(f32[2,576]{1,0:T(2,128)} %copy-done.81) | copy-start | bytes 13828
  221.9 19.5 %copy-start.118 = (f32[384]{0:T(512)S(1)}, f32[384]{0:T(512)}, u32[]{:S(2)}) copy-start(f32[384]{0:T(512)} %copy-done.116) | copy-start | bytes 4612
  226.1 6.4 %collective-permute-start.4 = (f32[56,384]{1,0:T(8,128)S(1)}, f32[56,384]{1,0:T(8,128)S(1)}, u32[]{:S(2)}, u32[]{:S(2)}) collective-permute-start(f32[56,384]{1,0:T(8,128)S(1)} %dynamic-slice_bitcast_fusion.6), channel_id=1, source_target_pairs={{0,16},{4,20},{8,24},{12,28},{16,0},{20,4},{24,8},{28,12},{1,17},{... | collective-permute-start | bytes 258056 | tf_op jit(solution)/shard_map/ppermute | solution.py:112
  232.5 5.6 %collective-permute-start.5 = (f32[56,384]{1,0:T(8,128)S(1)}, f32[56,384]{1,0:T(8,128)S(1)}, u32[]{:S(2)}, u32[]{:S(2)}) collective-permute-start(f32[56,384]{1,0:T(8,128)S(1)} %bitcast_add_fusion.7), channel_id=1, source_target_pairs={{0,16},{4,20},{8,24},{12,28},{16,0},{20,4},{24,8},{28,12},{1,17},{... | collective-permute-start | bytes 258056 | tf_op jit(solution)/shard_map/ppermute | solution.py:112
  238.1 6.7 %collective-permute-start.6 = (f32[112,384]{1,0:T(8,128)S(1)}, f32[112,384]{1,0:T(8,128)S(1)}, u32[]{:S(2)}, u32[]{:S(2)}) collective-permute-start(f32[112,384]{1,0:T(8,128)S(1)} %pad_maximum_fusion.7), channel_id=1, source_target_pairs={{0,8},{4,12},{8,0},{12,4},{16,24},{20,28},{24,16},{28,20},{1,9},{5... | collective-permute-start | bytes 516104 | tf_op jit(solution)/shard_map/ppermute | solution.py:112
  244.9 7.3 %collective-permute-start.7 = (f32[224,384]{1,0:T(8,128)S(1)}, f32[224,384]{1,0:T(8,128)S(1)}, u32[]{:S(2)}, u32[]{:S(2)}) collective-permute-start(f32[224,384]{1,0:T(8,128)S(1)} %pad_maximum_fusion.5), channel_id=1, source_target_pairs={{0,4},{4,0},{8,12},{12,8},{16,20},{20,16},{24,28},{28,24},{1,5},{5... | collective-permute-start | bytes 1032200 | tf_op jit(solution)/shard_map/ppermute | solution.py:112
  248.4 23.3 %collective-permute-start.9 = (f32[1,768,384]{2,1,0:T(8,128)S(1)}, f32[1,768,384]{2,1,0:T(8,128)S(1)}, u32[]{:S(2)}, u32[]{:S(2)}) collective-permute-start(f32[1,768,384]{2,1,0:T(8,128)S(1)} %constant_dynamic-slice_fusion.1), channel_id=1, source_target_pairs={{0,2},{1,3},{2,0},{3,1},{4,6},{5,7},{6,4},{7,5},{8,10},{9,11},{10,... | collective-permute-start | bytes 3538952 | tf_op jit(solution)/shard_map/ppermute | solution.py:112
  252.2 20.6 %collective-permute-start.16 = (f32[1,64,384]{2,1,0:T(8,128)S(1)}, f32[1,64,384]{2,1,0:T(8,128)S(1)}, u32[]{:S(2)}, u32[]{:S(2)}) collective-permute-start(f32[1,64,384]{2,1,0:T(8,128)S(1)} %slice_bitcast_fusion), channel_id=1, source_target_pairs={{0,2},{1,3},{2,0},{3,1},{4,6},{5,7},{6,4},{7,5},{8,10},{9,11},{10,... | collective-permute-start | bytes 294920 | tf_op jit(solution)/shard_map/ppermute | solution.py:112
  254.5 104.8 %copy-start.38 = (f32[96,384]{1,0:T(8,128)}, f32[96,384]{1,0:T(8,128)S(1)}, u32[]{:S(2)}) copy-start(f32[96,384]{1,0:T(8,128)S(1)} %get-tuple-element.234) | copy-start | bytes 442372
  255.3 106.0 %copy-start.27 = (f32[384,288]{0,1:T(8,128)}, f32[384,288]{0,1:T(8,128)S(1)}, u32[]{:S(2)}) copy-start(f32[384,288]{0,1:T(8,128)S(1)} %get-tuple-element.236) | copy-start | bytes 1327108
  272.0 9.9 %collective-permute-start.10 = (f32[384,384]{1,0:T(8,128)S(1)}, f32[384,384]{1,0:T(8,128)S(1)}, u32[]{:S(2)}, u32[]{:S(2)}) collective-permute-start(f32[384,384]{1,0:T(8,128)S(1)} %dynamic-slice_bitcast_fusion.1), channel_id=1, source_target_pairs={{0,4},{4,0},{8,12},{12,8},{16,20},{20,16},{24,28},{28,24},{1,5},{5... | collective-permute-start | bytes 1769480 | tf_op jit(solution)/shard_map/ppermute | solution.py:112
  272.8 1.5 collective-permute-start.17
  273.4 9.7 %collective-permute-start.18 = (f32[384,384]{1,0:T(8,128)S(1)}, f32[384,384]{1,0:T(8,128)S(1)}, u32[]{:S(2)}, u32[]{:S(2)}) collective-permute-start(f32[384,384]{1,0:T(8,128)S(1)} %get-tuple-element.293), channel_id=1, source_target_pairs={{0,1},{1,0},{2,3},{3,2},{4,5},{5,4},{6,7},{7,6},{8,9},{9,8},{10,11... | collective-permute-start | bytes 1769480 | tf_op jit(solution)/shard_map/ppermute | solution.py:112
  282.0 7.4 %collective-permute-start.11 = (f32[192,384]{1,0:T(8,128)S(1)}, f32[192,384]{1,0:T(8,128)S(1)}, u32[]{:S(2)}, u32[]{:S(2)}) collective-permute-start(f32[192,384]{1,0:T(8,128)S(1)} %dynamic-slice_bitcast_fusion.3), channel_id=1, source_target_pairs={{0,8},{4,12},{8,0},{12,4},{16,24},{20,28},{24,16},{28,20},{1,9},{5... | collective-permute-start | bytes 884744 | tf_op jit(solution)/shard_map/ppermute | solution.py:112
  283.3 14.7 %collective-permute-start.19 = (f32[384,384]{1,0:T(8,128)S(1)}, f32[384,384]{1,0:T(8,128)S(1)}, u32[]{:S(2)}, u32[]{:S(2)}) collective-permute-start(f32[384,384]{1,0:T(8,128)S(1)} %select_add_fusion.11), channel_id=1, source_target_pairs={{0,2},{1,3},{2,0},{3,1},{4,6},{5,7},{6,4},{7,5},{8,10},{9,11},{10,... | collective-permute-start | bytes 1769480 | tf_op jit(solution)/shard_map/ppermute | solution.py:112
  289.5 7.8 %collective-permute-start.12 = (f32[96,384]{1,0:T(8,128)S(1)}, f32[96,384]{1,0:T(8,128)S(1)}, u32[]{:S(2)}, u32[]{:S(2)}) collective-permute-start(f32[96,384]{1,0:T(8,128)S(1)} %dynamic-slice_bitcast_fusion.5), channel_id=1, source_target_pairs={{0,16},{4,20},{8,24},{12,28},{16,0},{20,4},{24,8},{28,12},{1,17},{... | collective-permute-start | bytes 442376 | tf_op jit(solution)/shard_map/ppermute | solution.py:112
  297.3 7.7 %collective-permute-start.13 = (f32[96,384]{1,0:T(8,128)S(1)}, f32[96,384]{1,0:T(8,128)S(1)}, u32[]{:S(2)}, u32[]{:S(2)}) collective-permute-start(f32[96,384]{1,0:T(8,128)S(1)} %bitcast_add_fusion.6), channel_id=1, source_target_pairs={{0,16},{4,20},{8,24},{12,28},{16,0},{20,4},{24,8},{28,12},{1,17},{... | collective-permute-start | bytes 442376 | tf_op jit(solution)/shard_map/ppermute | solution.py:112
  305.0 6.8 %collective-permute-start.14 = (f32[192,384]{1,0:T(8,128)S(1)}, f32[192,384]{1,0:T(8,128)S(1)}, u32[]{:S(2)}, u32[]{:S(2)}) collective-permute-start(f32[192,384]{1,0:T(8,128)S(1)} %pad_maximum_fusion.6), channel_id=1, source_target_pairs={{0,8},{4,12},{8,0},{12,4},{16,24},{20,28},{24,16},{28,20},{1,9},{5... | collective-permute-start | bytes 884744 | tf_op jit(solution)/shard_map/ppermute | solution.py:112
  311.9 9.9 %collective-permute-start.15 = (f32[384,384]{1,0:T(8,128)S(1)}, f32[384,384]{1,0:T(8,128)S(1)}, u32[]{:S(2)}, u32[]{:S(2)}) collective-permute-start(f32[384,384]{1,0:T(8,128)S(1)} %pad_maximum_fusion.2), channel_id=1, source_target_pairs={{0,4},{4,0},{8,12},{12,8},{16,20},{20,16},{24,28},{28,24},{1,5},{5... | collective-permute-start | bytes 1769480 | tf_op jit(solution)/shard_map/ppermute | solution.py:112
  323.9 43.7 %copy-start.26 = (f32[384,384]{1,0:T(8,128)}, f32[384,384]{1,0:T(8,128)S(1)}, u32[]{:S(2)}) copy-start(f32[384,384]{1,0:T(8,128)S(1)} %get-tuple-element.228) | copy-start | bytes 1769476
  324.7 2.3 collective-permute-start.21
  327.1 15.8 %collective-permute-start.22 = (f32[384,384]{1,0:T(8,128)S(1)}, f32[384,384]{1,0:T(8,128)S(1)}, u32[]{:S(2)}, u32[]{:S(2)}) collective-permute-start(f32[384,384]{1,0:T(8,128)S(1)} %select_add_fusion.10), channel_id=1, source_target_pairs={{0,2},{1,3},{2,0},{3,1},{4,6},{5,7},{6,4},{7,5},{8,10},{9,11},{10,... | collective-permute-start | bytes 1769480 | tf_op jit(solution)/shard_map/ppermute | solution.py:112
  330.8 28.5 %collective-permute-start.20 = (f32[384,384]{1,0:T(8,128)S(1)}, f32[384,384]{1,0:T(8,128)}, u32[]{:S(2)}, u32[]{:S(2)}) collective-permute-start(f32[384,384]{1,0:T(8,128)S(1)} %fusion.196), channel_id=1, source_target_pairs={{0,1},{1,0},{2,3},{3,2},{4,5},{5,4},{6,7},{7,6},{8,9},{9,8},{10,11... | collective-permute-start | bytes 1769480 | tf_op jit(solution)/shard_map/ppermute | solution.py:112
  357.9 7.0 %collective-permute-start.23 = (f32[384,384]{1,0:T(8,128)S(1)}, f32[384,384]{1,0:T(8,128)}, u32[]{:S(2)}, u32[]{:S(2)}) collective-permute-start(f32[384,384]{1,0:T(8,128)S(1)} %fusion.207), channel_id=1, source_target_pairs={{0,1},{1,0},{2,3},{3,2},{4,5},{5,4},{6,7},{7,6},{8,9},{9,8},{10,11... | collective-permute-start | bytes 1769480 | tf_op jit(solution)/shard_map/ppermute | solution.py:112
  (145 other events, 620.6 us)
